TPU v7x, 32 devices: a whole 2x2x4 slice. The times are simulated.
32 devices in a mesh: groups: 2 (over y), seq: 4 (over z), head: 2 (over x), sub: 2 (over core).
Axes of the slice: x: 2, y: 2, z: 4, core: 2. Of those that a mesh axis runs over, the one named last changes fastest.
Arguments:
- tokens: int32 [3, 4096], P(None, ('groups', 'seq')), parts along dimension 1, may hold values from 0 to 1023
- masked: int32 [4096], P(('groups', 'seq')), parts along dimension 0, may hold values 0 or 1
- used_frames: int32 [2], P('groups'), parts along dimension 0, may hold values from 1024 to 2048
- tables: bfloat16 [3, 1024, 1024], P(None, None, ('head', 'sub')), may hold values from -6 to 6
- mask_vec: bfloat16 [1024], P(('head', 'sub')), may hold values from -6 to 6
- attn_in: bfloat16 [3, 1024, 512], P(None, None, ('head', 'sub')), may hold values from -0.1875 to 0.1875
- head_temp: float32 [8], P(('head', 'sub')), may hold values from 12 to 28
- attn_out: bfloat16 [512, 1024], P(('head', 'sub')), may hold values from -0.25 to 0.25
- conv_in: bfloat16 [2, 1024, 1024], P(None, None, ('head', 'sub')), may hold values from -0.1875 to 0.1875
- conv_kernel: float32 [31, 1024], P(None, ('head', 'sub')), may hold values from -1 to 1
- conv_out: bfloat16 [1024, 1024], P(('head', 'sub')), may hold values from -0.1875 to 0.1875
- voc_in: bfloat16 [1024, 512], P(('head', 'sub')), may hold values from -0.1875 to 0.1875
- voc_kernel: float32 [7, 512], replicated, may hold values from -2 to 2
- voc_up: bfloat16 [512, 1536], P(('head', 'sub')), may hold values from -0.25 to 0.25
- voc_down: bfloat16 [1536, 512], P(('head', 'sub')), may hold values from -0.15625 to 0.15625
- voc_head: bfloat16 [512, 1282], P(('head', 'sub')), may hold values from -0.25 to 0.25
- head_bias: float32 [1282], replicated, may hold values from 0.5 to 2.5
Outputs:
- features: bfloat16 [4096, 1024], P(('groups', 'seq', 'head', 'sub')), parts along dimension 0
- waveform: float32 [1310720], P(('groups', 'seq', 'head', 'sub')), parts along dimension 0
There are 2 independent parts, one for each index of `groups`. A program takes and returns all parts, laid end to end along the dimension named above; an argument that names none is the same for every part. Nothing has to cross between parts.
All inputs are finite; a program needn't handle non-finite values. No bound on the sum of `masked` on one device may be relied on, other than what follows from the above.
Results may differ from a plain program's by a relative error of at most 0.02.
Values may be sent and summed in bfloat16 or wider, within the bound.
A program may use at most 64 MiB of HBM per device.

v0:
```python
import math
import jax
import jax.numpy as jnp
from jax import lax
from jax.sharding import PartitionSpec as P

HOP = 320


def with_halo(x, sides, width):
    for axis, dim in sides:
        size, length = (lax.axis_size(axis), x.shape[dim])
        up = [(i, (i + 1) % size) for i in range(size - 1)]
        down = [(j, i) for i, j in up]
        last = lax.slice_in_dim(x, length - width, length, axis=dim)
        initial = lax.slice_in_dim(x, 0, width, axis=dim)
        before = lax.ppermute(last, axis, up)
        after = lax.ppermute(initial, axis, down)
        x = jnp.concatenate([before, x, after], axis=dim)
    return x


def layer_norm(values):
    average = jnp.mean(values, axis=-1, keepdims=True)
    centered = values - average
    return centered * lax.rsqrt(jnp.mean(centered * centered, axis=-1, keepdims=True) + 1e-05)


def unit_heads(projected, head_count):
    row_count = projected.shape[0]
    split_heads = projected.reshape(row_count, head_count, projected.shape[1] // head_count)
    scaled = split_heads * lax.rsqrt(
        jnp.sum(split_heads * split_heads, axis=-1, keepdims=True) + 1e-06
    )
    return scaled.astype(jnp.bfloat16)


def depthwise(kernel, padded_rows):
    tap_count = kernel.shape[0]
    out_rows = padded_rows.shape[0] - tap_count + 1
    result = jnp.zeros((out_rows, padded_rows.shape[1]), jnp.float32)
    for offset in range(tap_count):
        result = result + kernel[offset] * padded_rows[offset : offset + out_rows].astype(
            jnp.float32
        )
    return result


def attend_block(
    paired_sums,
    key_tile_rows,
    value_tile_rows,
    leading_row,
    query_normalized,
    similarity_sharpness,
    frame_ceiling,
):
    weighted, normalizer = paired_sums
    row_count = key_tile_rows.shape[0]
    angular_similarity = jnp.einsum(
        "qhd,khd->hqk", query_normalized, key_tile_rows, preferred_element_type=jnp.float32
    )
    token_position = leading_row + lax.broadcasted_iota(jnp.int32, (1, 1, row_count), 2)
    attention_probabilities = jnp.where(
        token_position < frame_ceiling,
        jnp.exp(similarity_sharpness[:, None, None] * (angular_similarity - 1.0)),
        0.0,
    )
    normalizer = normalizer + jnp.sum(attention_probabilities, axis=2).T
    weighted = weighted + jnp.einsum(
        "hqk,khd->qhd",
        attention_probabilities.astype(jnp.bfloat16),
        value_tile_rows,
        preferred_element_type=jnp.float32,
    )
    return (weighted, normalizer)


def synthesis_tables(bin_count, fft_size):
    bin_ids = lax.broadcasted_iota(jnp.int32, (bin_count, fft_size), 0)
    sample_ids = lax.broadcasted_iota(jnp.int32, (bin_count, fft_size), 1)
    phase_angle = 2.0 * math.pi / fft_size * (bin_ids * sample_ids % fft_size).astype(jnp.float32)
    edge_bin = (bin_ids == 0) | (bin_ids == bin_count - 1)
    factor = jnp.where(edge_bin, 1.0, 2.0) / fft_size
    cos_table = factor * jnp.cos(phase_angle)
    sin_table = jnp.where(edge_bin, 0.0, -factor * jnp.sin(phase_angle))
    return jnp.concatenate([cos_table, sin_table], axis=0)


def local(
    tokens,
    masked,
    used_frames,
    tables,
    mask_vec,
    attn_in,
    head_temp,
    attn_out,
    conv_in,
    conv_kernel,
    conv_out,
    voc_in,
    voc_kernel,
    voc_up,
    voc_down,
    voc_head,
    head_bias,
):
    frame_count = tokens.shape[1]
    group_count = lax.axis_size(("head", "sub"))
    group_index = lax.axis_index(("head", "sub"))
    seq_index = lax.axis_index("seq")
    slab_rows = frame_count // group_count
    frame_ceiling = used_frames[0]
    total_frames = frame_count * lax.axis_size("seq")
    code_ids = lax.broadcasted_iota(jnp.int32, (frame_count, tables.shape[1]), 1)
    masked_rows = masked == 1
    embedded = masked_rows.astype(jnp.float32)[:, None] * mask_vec.astype(jnp.float32)[None, :]
    for rvq_level in range(3):
        matches = tokens[rvq_level][:, None] == code_ids
        if rvq_level == 2:
            matches = matches & jnp.logical_not(masked_rows)[:, None]
        embedded = embedded + jnp.dot(
            matches.astype(jnp.bfloat16), tables[rvq_level], preferred_element_type=jnp.float32
        )
    embedded = embedded.astype(jnp.bfloat16)
    inputs, voc_in_full, voc_up_full, voc_down_full, voc_head_full = (
        lax.all_gather(embedded, ("head", "sub"), axis=1, tiled=True),
        lax.all_gather(voc_in, ("head", "sub"), axis=0, tiled=True),
        lax.all_gather(voc_up, ("head", "sub"), axis=0, tiled=True),
        lax.all_gather(voc_down, ("head", "sub"), axis=0, tiled=True),
        lax.all_gather(voc_head, ("head", "sub"), axis=0, tiled=True),
    )
    normed = layer_norm(inputs.astype(jnp.float32)).astype(jnp.bfloat16)
    local_heads = head_temp.shape[0]
    query_normalized = unit_heads(
        jnp.dot(normed, attn_in[0], preferred_element_type=jnp.float32), local_heads
    )
    key_unit = unit_heads(
        jnp.dot(normed, attn_in[1], preferred_element_type=jnp.float32), local_heads
    ).reshape(frame_count, -1)
    value_rows = jnp.dot(normed, attn_in[2], preferred_element_type=jnp.float32).astype(
        jnp.bfloat16
    )
    head_size = value_rows.shape[1] // local_heads
    start_pair = (
        jnp.zeros((frame_count, local_heads, head_size), jnp.float32),
        jnp.zeros((frame_count, local_heads), jnp.float32),
    )
    paired_sums = start_pair
    key_piece = lax.all_gather(key_unit, "seq", axis=0, tiled=True)
    value_piece = lax.all_gather(value_rows, "seq", axis=0, tiled=True)
    row_count = key_piece.shape[0]
    key_heads = key_piece.reshape(row_count, local_heads, head_size)
    value_heads = value_piece.reshape(row_count, local_heads, head_size)
    block_count = row_count // 512

    def scan_step(inner_pair, block_item):
        key_tile_rows, value_tile_rows, block_index = block_item
        return (
            attend_block(
                inner_pair,
                key_tile_rows,
                value_tile_rows,
                block_index * 512,
                query_normalized,
                head_temp,
                frame_ceiling,
            ),
            None,
        )

    block_items = (
        key_heads.reshape(block_count, 512, local_heads, head_size),
        value_heads.reshape(block_count, 512, local_heads, head_size),
        jnp.arange(block_count, dtype=jnp.int32),
    )
    paired_sums, _unused = lax.scan(scan_step, paired_sums, block_items)
    weighted, normalizer = paired_sums
    attended = (weighted / normalizer[:, :, None]).reshape(frame_count, -1).astype(jnp.bfloat16)
    head_part = jnp.dot(attended, attn_out, preferred_element_type=jnp.float32)
    fft_size = 2 * (head_bias.shape[0] // 2 - 1)
    intersection = fft_size // HOP
    half_voc = voc_kernel.shape[0] // 2
    vocoder_rim = half_voc + intersection // 2
    conv_reach = conv_kernel.shape[0] // 2 + vocoder_rim
    window_rows = slab_rows + 2 * vocoder_rim
    stream = inputs.astype(jnp.float32) + lax.psum(
        head_part.astype(jnp.bfloat16), ("head", "sub")
    ).astype(jnp.float32)
    stream_rims = with_halo(stream.astype(jnp.bfloat16), (("seq", 0),), conv_reach).astype(
        stream.dtype
    )
    conv_normed = layer_norm(stream_rims).astype(jnp.bfloat16)
    residual_window = lax.dynamic_slice_in_dim(
        stream_rims, group_index * slab_rows + conv_reach - vocoder_rim, window_rows, 0
    )
    gate_value = jnp.dot(conv_normed, conv_in[0], preferred_element_type=jnp.float32)
    gate_signal = jnp.dot(conv_normed, conv_in[1], preferred_element_type=jnp.float32)
    gated_rows = (gate_value * jax.nn.sigmoid(gate_signal)).astype(jnp.bfloat16)
    depth_rows = depthwise(conv_kernel, gated_rows)
    activated = (depth_rows * jax.nn.sigmoid(depth_rows)).astype(jnp.bfloat16)
    windows = jnp.stack(
        [
            activated[member * slab_rows : member * slab_rows + window_rows]
            for member in range(group_count)
        ]
    )
    partial_out = jnp.einsum("gsc,cd->gsd", windows, conv_out, preferred_element_type=jnp.float32)
    conv_sum = lax.psum_scatter(
        partial_out.astype(jnp.bfloat16), ("head", "sub"), scatter_dimension=0, tiled=True
    ).astype(jnp.float32)[0]
    block_norm = layer_norm(residual_window + conv_sum).astype(jnp.bfloat16)
    feature_out = block_norm[vocoder_rim : vocoder_rim + slab_rows]
    first_frame = seq_index * frame_count + group_index * slab_rows - vocoder_rim
    frame_ids = first_frame + lax.broadcasted_iota(jnp.int32, (window_rows, 1), 0)
    live_rows = (frame_ids >= 0) & (frame_ids < frame_ceiling)
    base_rows = layer_norm(
        jnp.where(
            live_rows, jnp.dot(block_norm, voc_in_full, preferred_element_type=jnp.float32), 0.0
        )
    )
    vdepth = depthwise(voc_kernel, base_rows)
    voc_rows = vdepth.shape[0]
    inner_rows = layer_norm(vdepth).astype(jnp.bfloat16)
    hidden = jax.nn.gelu(
        jnp.dot(inner_rows, voc_up_full, preferred_element_type=jnp.float32), approximate=False
    ).astype(jnp.bfloat16)
    refined = base_rows[half_voc : half_voc + voc_rows] + jnp.dot(
        hidden, voc_down_full, preferred_element_type=jnp.float32
    )
    head_input = layer_norm(refined).astype(jnp.bfloat16)
    spectrum = jnp.dot(head_input, voc_head_full, preferred_element_type=jnp.float32) + head_bias
    bin_count = spectrum.shape[1] // 2
    magnitude = jnp.minimum(jnp.exp(spectrum[:, :bin_count]), 100.0)
    phase_rows = spectrum[:, bin_count:]
    coefficients = jnp.concatenate(
        [magnitude * jnp.cos(phase_rows), magnitude * jnp.sin(phase_rows)], axis=1
    )
    wave_rows = jnp.dot(
        coefficients, synthesis_tables(bin_count, fft_size), precision=lax.Precision.HIGHEST
    )
    sample_ids = lax.broadcasted_iota(jnp.int32, (fft_size,), 0).astype(jnp.float32)
    hann_window = 0.5 - 0.5 * jnp.cos(2.0 * math.pi / fft_size * sample_ids)
    wave_ids = first_frame + half_voc + lax.broadcasted_iota(jnp.int32, (voc_rows, 1), 0)
    exists = ((wave_ids >= 0) & (wave_ids < total_frames)).astype(jnp.float32)
    framed = (wave_rows * hann_window[None, :] * exists).reshape(voc_rows, intersection, HOP)
    env_rows = (exists * (hann_window * hann_window)[None, :]).reshape(voc_rows, intersection, HOP)
    audio_sum = jnp.zeros((slab_rows, HOP), jnp.float32)
    energy = jnp.zeros((slab_rows, HOP), jnp.float32)
    for quarter in range(intersection):
        begin = intersection - quarter
        audio_sum = audio_sum + framed[begin : begin + slab_rows, quarter]
        energy = energy + env_rows[begin : begin + slab_rows, quarter]
    waveform = (audio_sum / energy).reshape(slab_rows * HOP)
    return (feature_out, waveform)


def solution(mesh):
    in_specs = (
        P(None, ("groups", "seq")),
        P(("groups", "seq")),
        P("groups"),
        P(None, None, ("head", "sub")),
        P(("head", "sub")),
        P(None, None, ("head", "sub")),
        P(("head", "sub")),
        P(("head", "sub"), None),
        P(None, None, ("head", "sub")),
        P(None, ("head", "sub")),
        P(("head", "sub"), None),
        P(("head", "sub"), None),
        P(),
        P(("head", "sub"), None),
        P(("head", "sub"), None),
        P(("head", "sub"), None),
        P(),
    )
    out_specs = (P(("groups", "seq", "head", "sub"), None), P(("groups", "seq", "head", "sub")))
    return jax.shard_map(local, mesh=mesh, in_specs=in_specs, out_specs=out_specs, check_vma=False)
```

profile of v0, /device:TPU:0, one launch (start us, length us, event | category | flops | bytes accessed | tf_op | source)
XLA Modules:
  0.0 276.2 jit_solution(7080855097597714248)
XLA Ops:
  12.6 2.3 fusion.41
  16.1 18.6 %all-gather.6.cloned.1.call-done = bf16[512,1024]{1,0:T(8,128)(2,1)} async-done(((bf16[512,256]{1,0:T(8,128)(2,1)}), bf16[512,1024]{1,0:T(8,128)(2,1)}) %all-gather.6.cloned.1.call-update) | async-done | bytes 1048592 | tf_op jit(solution)/shard_map/all_gather | solution.py:128
  40.1 16.0 %all_gather.23 = bf16[2048,128]{0,1:T(8,128)(2,1)S(1)} all-gather(bf16[512,128]{0,1:T(8,128)(2,1)S(1)} %bitcast.157), channel_id=1, replica_groups=mesh['groups'=2,'seq'=4,'head'=2,'sub'=2] {'seq'}, dimensions={0}, use_global_device_ids=true | all-gather | bytes 655360 | tf_op jit(solution)/shard_map/all_gather | solution.py:151
  57.3 1.9 copy.28
  59.2 2.1 multiply_reduce_fusion.5
  61.4 16.1 %all_gather.22 = bf16[2048,128]{1,0:T(8,128)(2,1)S(1)} all-gather(bf16[512,128]{1,0:T(8,128)(2,1)S(1)} %convolution_convert_fusion.2), channel_id=1, replica_groups=mesh['groups'=2,'seq'=4,'head'=2,'sub'=2] {'seq'}, dimensions={0}, use_global_device_ids=true | all-gather | bytes 655360 | tf_op jit(solution)/shard_map/all_gather | solution.py:152
  79.6 15.6 %while.15 = (s32[]{:T(128)}, f32[512,2,64]{0,2,1:T(8,128)S(1)}, f32[512,2]{0,1:T(2,128)S(1)}, bf16[4,512,2,64]{1,3,2,0:T(8,128)(2,1)S(1)}, s32[4]{0:T(128)S(1)},...) while((s32[]{:T(128)}, f32[512,2,64]{0,2,1:T(8,128)S(1)}, ...), condition=%wide.region_6.7_spmd.clone, body=%wide.region_4.6_spmd.clone.sunk | while | flops 136972288 | bytes 3032748 | solution.py:178
  95.3 2.4 convolution_convert_fusion.1
  97.9 36.0 %all-reduce.2.cloned.1.call-done = bf16[512,1024]{1,0:T(8,128)(2,1)} async-done(((bf16[512,1024]{1,0:T(8,128)(2,1)}), bf16[512,1024]{1,0:T(8,128)(2,1)}) %all-reduce.2.cloned.1.call-update) | async-done | bytes 1048592 | tf_op jit(solution)/shard_map/psum | solution.py:188
  133.9 1.7 fusion.26
  135.6 3.4 %collective-permute-start = (bf16[20,1024]{1,0:T(8,128)(2,1)S(1)}, bf16[20,1024]{1,0:T(8,128)(2,1)S(1)}, u32[]{:S(2)}, u32[]{:S(2)}) collective-permute-start(bf16[20,1024]{1,0:T(8,128)(2,1)S(1)} %get-tuple-element.190), channel_id=1, source_target_pairs={{0,4},{4,8},{8,12},{1,5},{5,9},{9,13},{2,6},{6,10},{10,14},{3,7},{... | collective-permute-start | bytes 122888 | tf_op jit(solution)/shard_map/ppermute | solution.py:17
  140.8 4.3 %collective-permute-done.1 = bf16[20,1024]{1,0:T(8,128)(2,1)S(1)} collective-permute-done((bf16[20,1024]{1,0:T(8,128)(2,1)S(1)}, bf16[20,1024]{1,0:T(8,128)(2,1)S(1)}, u32[]{:S(2)}, u32[]{:S(2)}) %collective-permute-start.1) | collective-permute-done | bytes 40992 | tf_op jit(solution)/shard_map/ppermute | solution.py:18
  147.6 2.3 multiply_convert_fusion.2
  155.0 15.1 %multiply_select_fusion = (f32[641,1280]{1,0:T(8,128)}, f32[641,1280]{1,0:T(8,128)}) fusion(f32[641]{0:T(1024)S(1)} %fusion.133, pred[641]{0:T(1024)(128)(4,1)S(1)} %fusion.132, f32[641]{0:T(1024)S(1)} %select_multiply_fusion), kind=kLoop, calls=%fused_computation.20 | loop fusion | flops 9845760 | bytes 6569609 | tf_op jit(solution)/shard_map/jit(_where)/select_n | solution.py:86
  170.1 1.8 fusion.166
  171.9 4.9 %reduce-scatter.2.cloned.1.call-done = bf16[1,138,1024]{2,1,0:T(8,128)(2,1)} async-done(((bf16[4,138,1024]{2,1,0:T(8,128)(2,1)}), bf16[1,138,1024]{2,1,0:T(8,128)(2,1)}) %reduce-scatter.2.cloned.1.call-update) | async-done | bytes 282640 | tf_op jit(solution)/shard_map/reduce_scatter | solution.py:210
  180.9 14.1 %all-gather.8.cloned.1.call-done = bf16[1024,512]{1,0:T(8,128)(2,1)} async-done(((bf16[256,512]{1,0:T(8,128)(2,1)}), bf16[1024,512]{1,0:T(8,128)(2,1)}) %all-gather.8.cloned.1.call-update) | async-done | bytes 1048592 | tf_op jit(solution)/shard_map/all_gather | solution.py:129
  198.3 17.7 %all-gather.10.cloned.1.call-done = bf16[512,1536]{1,0:T(8,128)(2,1)} async-done(((bf16[128,1536]{1,0:T(8,128)(2,1)}), bf16[512,1536]{1,0:T(8,128)(2,1)}) %all-gather.10.cloned.1.call-update) | async-done | bytes 1572880 | tf_op jit(solution)/shard_map/all_gather | solution.py:130
  216.0 21.1 %all-gather.12.cloned.1.call-done = bf16[1536,512]{1,0:T(8,128)(2,1)} async-done(((bf16[384,512]{1,0:T(8,128)(2,1)}), bf16[1536,512]{1,0:T(8,128)(2,1)}) %all-gather.12.cloned.1.call-update) | async-done | bytes 1572880 | tf_op jit(solution)/shard_map/all_gather | solution.py:131
  237.1 4.3 %fusion.178 = (f32[132]{0:T(256)S(1)}, f32[132,512]{1,0:T(8,128)S(1)}) fusion(bf16[1536,512]{1,0:T(8,128)(2,1)} %all-gather.12.cloned.1.call-done, bf16[512,1536]{1,0:T(8,128)(2,1)} %all-gather.10.cloned.1.call-done, f32[132,512]{1,0:T(8,128)S(1)} %get-tuple-element.185, f32[132]{0:T(256)S(1)} %add_rsqrt_fusion.5, f32[132]{0:T(256)S(1)} %broadcast_multiply_fusion.4, ...), kind=kOutput, calls=%fused_computation.260 | convolution fusion | flops 428752768 | bytes 3958320 | tf_op jit(solution)/shard_map/dot_general | solution.py:229
  241.6 15.4 %all-gather.14.cloned.1.call-done = bf16[512,1282]{0,1:T(8,128)(2,1)} async-done(((bf16[128,1282]{0,1:T(8,128)(2,1)}), bf16[512,1282]{0,1:T(8,128)(2,1)}) %all-gather.14.cloned.1.call-update) | async-done | bytes 1312784 | tf_op jit(solution)/shard_map/all_gather | solution.py:132
  257.0 2.1 convolution_add_fusion
  259.2 1.9 cosine_multiply_fusion.1
  261.1 6.2 %fusion.19 = f32[132,1280]{1,0:T(8,128)S(1)} fusion(f32[641,1280]{1,0:T(8,128)S(1)} %copy-done.2, f32[641,1280]{1,0:T(8,128)} %get-tuple-element.254, f32[132,641]{1,0:T(8,128)S(1)} %get-tuple-element.199, f32[132,641]{1,0:T(8,128)S(1)} %get-tuple-element.198, f32[132]{0:T(256)S(1)} %and_convert_fusion, f32[1280]{0:T(1024)S(1)} %multiply_subtract_fusion), kind=kOutput, calls=%fused_computation.31 | convolution fusion | flops 2601428736 | bytes 7922224 | tf_op jit(solution)/shard_map/dot_general | solution.py:240
  (123 shorter events, 46.3 us)
Async XLA Ops:
  7.2 142.8 %copy-start = (bf16[256,1024]{1,0:T(8,128)(2,1)S(1)}, bf16[256,1024]{1,0:T(8,128)(2,1)}, u32[]{:S(2)}) copy-start(bf16[256,1024]{1,0:T(8,128)(2,1)} %param.29) | copy-start | bytes 1572868
  7.2 27.5 %all-gather.6.cloned.1.call-start = ((), (), s32[]{:S(2)}) async-start(), calls=%async_computation.1 | async-start | bytes 1310720 | tf_op jit(solution)/shard_map/all_gather | solution.py:128
  11.0 4.1 %copy-start.3 = (bf16[3,1024,128]{2,1,0:T(8,128)(2,1)S(1)}, bf16[3,1024,128]{2,1,0:T(8,128)(2,1)}, u32[]{:S(2)}) copy-start(bf16[3,1024,128]{2,1,0:T(8,128)(2,1)} %param.24) | copy-start | bytes 2359300
  14.9 119.0 %all-reduce.2.cloned.1.call-start = ((), (), s32[]{:S(2)}) async-start(), calls=%async_computation.2 | async-start | bytes 2097152 | tf_op jit(solution)/shard_map/psum | solution.py:188
  34.6 3.2 %copy-start.1 = (bf16[512,1024]{1,0:T(8,128)(2,1)S(1)}, bf16[512,1024]{1,0:T(8,128)(2,1)}, u32[]{:S(2)}) copy-start(bf16[512,1024]{1,0:T(8,128)(2,1)} %all-gather.6.cloned.1.call-done) | copy-start | bytes 3145732
  61.4 18.3 %copy-start.8 = (f32[2]{0:T(128)S(1)}, f32[2]{0:T(128)}, u32[]{:S(2)}) copy-start(f32[2]{0:T(128)} %param.25) | copy-start | bytes 28
  95.3 2.6 copy-start.4
  97.8 79.0 %reduce-scatter.2.cloned.1.call-start = ((), (), s32[]{:S(2)}) async-start(), calls=%async_computation.3 | async-start | bytes 1474560 | tf_op jit(solution)/shard_map/reduce_scatter | solution.py:210
  133.9 12.1 %copy-start.7 = (bf16[2,1024,256]{2,1,0:T(8,128)(2,1)S(1)}, bf16[2,1024,256]{2,1,0:T(8,128)(2,1)}, u32[]{:S(2)}) copy-start(bf16[2,1024,256]{2,1,0:T(8,128)(2,1)} %param.27) | copy-start | bytes 3145732
  135.6 5.1 %collective-permute-start = (bf16[20,1024]{1,0:T(8,128)(2,1)S(1)}, bf16[20,1024]{1,0:T(8,128)(2,1)S(1)}, u32[]{:S(2)}, u32[]{:S(2)}) collective-permute-start(bf16[20,1024]{1,0:T(8,128)(2,1)S(1)} %get-tuple-element.190), channel_id=1, source_target_pairs={{0,4},{4,8},{8,12},{1,5},{5,9},{9,13},{2,6},{6,10},{10,14},{3,7},{... | collective-permute-start | bytes 122888 | tf_op jit(solution)/shard_map/ppermute | solution.py:17
  139.0 6.0 %collective-permute-start.1 = (bf16[20,1024]{1,0:T(8,128)(2,1)S(1)}, bf16[20,1024]{1,0:T(8,128)(2,1)S(1)}, u32[]{:S(2)}, u32[]{:S(2)}) collective-permute-start(bf16[20,1024]{1,0:T(8,128)(2,1)S(1)} %get-tuple-element.191), channel_id=1, source_target_pairs={{4,0},{8,4},{12,8},{5,1},{9,5},{13,9},{6,2},{10,6},{14,10},{7,3},{... | collective-permute-start | bytes 122888 | tf_op jit(solution)/shard_map/ppermute | solution.py:18
  149.9 4.8 %copy-start.5 = (f32[7,512]{1,0:T(8,128)S(1)}, f32[7,512]{1,0:T(8,128)}, u32[]{:S(2)}) copy-start(f32[7,512]{1,0:T(8,128)} %param.31) | copy-start | bytes 43012
  151.5 43.5 %all-gather.8.cloned.1.call-start = ((), (), s32[]{:S(2)}) async-start(), calls=%async_computation.4 | async-start | bytes 1310720 | tf_op jit(solution)/shard_map/all_gather | solution.py:129
  152.0 64.0 %all-gather.10.cloned.1.call-start = ((), (), s32[]{:S(2)}) async-start(), calls=%async_computation.5 | async-start | bytes 1966080 | tf_op jit(solution)/shard_map/all_gather | solution.py:130
  152.6 84.5 %all-gather.12.cloned.1.call-start = ((), (), s32[]{:S(2)}) async-start(), calls=%async_computation.6 | async-start | bytes 1966080 | tf_op jit(solution)/shard_map/all_gather | solution.py:131
  153.2 103.8 %all-gather.14.cloned.1.call-start = ((), (), s32[]{:S(2)}) async-start(), calls=%async_computation.7 | async-start | bytes 1648640 | tf_op jit(solution)/shard_map/all_gather | solution.py:132
  198.3 58.8 %copy-start.6 = (f32[1282]{0:T(1024)S(1)}, f32[1282]{0:T(1024)}, u32[]{:S(2)}) copy-start(f32[1282]{0:T(1024)} %param.35) | copy-start | bytes 15388
  257.0 4.0 %copy-start.2 = (f32[641,1280]{1,0:T(8,128)S(1)}, f32[641,1280]{1,0:T(8,128)}, u32[]{:S(2)}) copy-start(f32[641,1280]{1,0:T(8,128)} %get-tuple-element.253) | copy-start | bytes 9845764
Sparse Core Ops, SparseCore 0:
  15.1 19.5 all-gather.5
  97.9 35.9 all-reduce.1
  151.6 25.1 reduce-scatter.1
  178.2 16.6 all-gather.7
  196.3 19.6 all-gather.9
  217.4 19.6 all-gather.11
  238.6 18.3 all-gather.13
where the time goes:
time: 277 us; the launch traced here: 276 us
  waiting for transfers between devices  135 us (49%)
  other arithmetic  38 us (14%)
  matrix products  37 us (13%)
  blocking collectives  32.1 us (12%)
  between operations  15.2 us (5%)
  local copies, waits for them, and re-layouts  11.3 us (4%)
  starting transfers between devices  5.14 us (2%)
  loops' own time  2.77 us (1%)
    psum x1, waiting for transfers between devices, local(): lax.psum(head_part.astype(jnp.bfloat16), ('head', 'sub'))  36 us
    all_gather x1, waiting for transfers between devices, local(): lax.all_gather(voc_down, ('head', 'sub'), axis=0, tiled=True)  21.1 us
    all_gather x1, waiting for transfers between devices, local(): lax.all_gather(embedded, ('head', 'sub'), axis=1, tiled=True)  18.6 us
    all_gather x1, waiting for transfers between devices, local(): lax.all_gather(voc_up, ('head', 'sub'), axis=0, tiled=True)  17.7 us
    all_gather x1, blocking collectives, local(): value_piece = lax.all_gather(value_rows, 'seq', axis=0, tiled=True)  16.1 us
    all_gather x1, blocking collectives, local(): key_piece = lax.all_gather(key_unit, 'seq', axis=0, tiled=True)  16 us
    all_gather x1, waiting for transfers between devices, local(): lax.all_gather(voc_head, ('head', 'sub'), axis=0, tiled=True)  15.4 us
    select_n x1, other arithmetic, synthesis_tables(): sin_table = jnp.where(edge_bin, 0.0, -factor * jnp.sin(phase_angle))  15.1 us
  transfers between devices with their start and end apart: 9, of which 9 were waited for; matrix products, arithmetic and copies ran while one was open for 11% of the time, Pallas kernels for 0%

commit v1 on v0

--- a/solution.py
+++ b/solution.py
@@ -185,8 +185,8 @@
     vocoder_rim = half_voc + intersection // 2
     conv_reach = conv_kernel.shape[0] // 2 + vocoder_rim
     window_rows = slab_rows + 2 * vocoder_rim
-    stream = inputs.astype(jnp.float32) + lax.psum(
-        head_part.astype(jnp.bfloat16), ("head", "sub")
+    stream = inputs.astype(jnp.float32) + jnp.sum(
+        lax.all_gather(head_part.astype(jnp.bfloat16), ("head", "sub")), axis=0
     ).astype(jnp.float32)
     stream_rims = with_halo(stream.astype(jnp.bfloat16), (("seq", 0),), conv_reach).astype(
         stream.dtype

time: 277 us -> 279 us (level)
  other arithmetic: 38 us -> 42.4 us
  waiting for transfers between devices: 135 us -> 132 us
    psum x1 -> x0, waiting for transfers between devices: 36 us -> none  [local(): lax.psum(head_part.astype(jnp.bfloat16), ('head', 'sub'))]
    all_gather x0 -> x1, waiting for transfers between devices: none -> 34.2 us  [local(): lax.all_gather(head_part.astype(jnp.bfloat16), ('head', 'sub'))]
    reduce_sum x0 -> x1, other arithmetic: none -> 4.39 us  [local(): jnp.sum(lax.all_gather(head_part.astype(jnp.bfloat16), ('head', 'sub')),...]
where the time goes in v1:
time: 279 us; the launch traced here: 278 us
  waiting for transfers between devices  132 us (47%)
  other arithmetic  42.4 us (15%)
  matrix products  37 us (13%)
  blocking collectives  32.1 us (12%)
  between operations  15.2 us (5%)
  local copies, waits for them, and re-layouts  11.3 us (4%)
  starting transfers between devices  5.14 us (2%)
    all_gather x1, waiting for transfers between devices, local(): lax.all_gather(head_part.astype(jnp.bfloat16), ('head', 'sub'))  34.2 us
    all_gather x1, waiting for transfers between devices, local(): lax.all_gather(voc_down, ('head', 'sub'), axis=0, tiled=True)  21.1 us
    all_gather x1, waiting for transfers between devices, local(): lax.all_gather(embedded, ('head', 'sub'), axis=1, tiled=True)  18.6 us
    all_gather x1, waiting for transfers between devices, local(): lax.all_gather(voc_up, ('head', 'sub'), axis=0, tiled=True)  17.7 us
    all_gather x1, blocking collectives, local(): value_piece = lax.all_gather(value_rows, 'seq', axis=0, tiled=True)  16.1 us
    all_gather x1, blocking collectives, local(): key_piece = lax.all_gather(key_unit, 'seq', axis=0, tiled=True)  16 us
    all_gather x1, waiting for transfers between devices, local(): lax.all_gather(voc_head, ('head', 'sub'), axis=0, tiled=True)  15.4 us
    select_n x1, other arithmetic, synthesis_tables(): sin_table = jnp.where(edge_bin, 0.0, -factor * jnp.sin(phase_angle))  15.1 us
  transfers between devices with their start and end apart: 9, of which 9 were waited for; matrix products, arithmetic and copies ran while one was open for 11% of the time, Pallas kernels for 0%

profile of v1, /device:TPU:0, one launch (start us, length us, event | category | flops | bytes accessed | tf_op | source)
XLA Modules:
  0.0 278.2 jit_solution(5725965116289755121)
XLA Ops:
  12.6 2.3 fusion.41
  16.1 18.6 %all-gather.8.cloned.1.call-done = bf16[512,1024]{1,0:T(8,128)(2,1)} async-done(((bf16[512,256]{1,0:T(8,128)(2,1)}), bf16[512,1024]{1,0:T(8,128)(2,1)}) %all-gather.8.cloned.1.call-update) | async-done | bytes 1048592 | tf_op jit(solution)/shard_map/all_gather | solution.py:128
  40.1 16.0 %all_gather.29 = bf16[2048,128]{0,1:T(8,128)(2,1)S(1)} all-gather(bf16[512,128]{0,1:T(8,128)(2,1)S(1)} %bitcast.159), channel_id=1, replica_groups=mesh['groups'=2,'seq'=4,'head'=2,'sub'=2] {'seq'}, dimensions={0}, use_global_device_ids=true | all-gather | bytes 655360 | tf_op jit(solution)/shard_map/all_gather | solution.py:151
  57.3 1.9 copy.28
  59.2 2.1 multiply_reduce_fusion.5
  61.4 16.1 %all_gather.28 = bf16[2048,128]{1,0:T(8,128)(2,1)S(1)} all-gather(bf16[512,128]{1,0:T(8,128)(2,1)S(1)} %convolution_convert_fusion.2), channel_id=1, replica_groups=mesh['groups'=2,'seq'=4,'head'=2,'sub'=2] {'seq'}, dimensions={0}, use_global_device_ids=true | all-gather | bytes 655360 | tf_op jit(solution)/shard_map/all_gather | solution.py:152
  79.6 15.6 %while.15 = (s32[]{:T(128)}, f32[512,2,64]{0,2,1:T(8,128)S(1)}, f32[512,2]{0,1:T(2,128)S(1)}, bf16[4,512,2,64]{1,3,2,0:T(8,128)(2,1)S(1)}, s32[4]{0:T(128)S(1)},...) while((s32[]{:T(128)}, f32[512,2,64]{0,2,1:T(8,128)S(1)}, ...), condition=%wide.region_6.7_spmd.clone, body=%wide.region_4.6_spmd.clone.sunk | while | flops 136972288 | bytes 3032748 | solution.py:178
  95.3 2.4 convolution_convert_fusion.1
  97.8 34.2 %all-gather.18.cloned.1.call-done = bf16[2048,1024]{1,0:T(8,128)(2,1)} async-done(((bf16[512,1024]{1,0:T(8,128)(2,1)}), bf16[2048,1024]{1,0:T(8,128)(2,1)}) %all-gather.18.cloned.1.call-update) | async-done | bytes 4194320 | tf_op jit(solution)/shard_map/all_gather | solution.py:189
  132.0 4.4 %reduce_sum.154 = bf16[512,1024]{1,0:T(8,128)(2,1)} reduce(bf16[4,512,1024]{2,1,0:T(8,128)(2,1)} %bitcast.156, bf16[]{:T(256)} %constant.72.clone.1), dimensions={0}, to_apply=%region_7.8 | reduce | flops 1572864 | bytes 5242882 | tf_op jit(solution)/shard_map/reduce_sum | solution.py:188
  138.1 3.4 %collective-permute-start = (bf16[20,1024]{1,0:T(8,128)(2,1)S(1)}, bf16[20,1024]{1,0:T(8,128)(2,1)S(1)}, u32[]{:S(2)}, u32[]{:S(2)}) collective-permute-start(bf16[20,1024]{1,0:T(8,128)(2,1)S(1)} %get-tuple-element.190), channel_id=1, source_target_pairs={{0,4},{4,8},{8,12},{1,5},{5,9},{9,13},{2,6},{6,10},{10,14},{3,7},{... | collective-permute-start | bytes 122888 | tf_op jit(solution)/shard_map/ppermute | solution.py:17
  143.3 4.3 %collective-permute-done.1 = bf16[20,1024]{1,0:T(8,128)(2,1)S(1)} collective-permute-done((bf16[20,1024]{1,0:T(8,128)(2,1)S(1)}, bf16[20,1024]{1,0:T(8,128)(2,1)S(1)}, u32[]{:S(2)}, u32[]{:S(2)}) %collective-permute-start.1) | collective-permute-done | bytes 40992 | tf_op jit(solution)/shard_map/ppermute | solution.py:18
  150.1 2.3 multiply_convert_fusion.2
  157.5 15.1 %multiply_select_fusion = (f32[641,1280]{1,0:T(8,128)}, f32[641,1280]{1,0:T(8,128)}) fusion(f32[641]{0:T(1024)S(1)} %fusion.133, pred[641]{0:T(1024)(128)(4,1)S(1)} %fusion.132, f32[641]{0:T(1024)S(1)} %select_multiply_fusion), kind=kLoop, calls=%fused_computation.20 | loop fusion | flops 9845760 | bytes 6569609 | tf_op jit(solution)/shard_map/jit(_where)/select_n | solution.py:86
  172.6 1.8 fusion.166
  174.4 4.4 %reduce-scatter.2.cloned.1.call-done = bf16[1,138,1024]{2,1,0:T(8,128)(2,1)} async-done(((bf16[4,138,1024]{2,1,0:T(8,128)(2,1)}), bf16[1,138,1024]{2,1,0:T(8,128)(2,1)}) %reduce-scatter.2.cloned.1.call-update) | async-done | bytes 282640 | tf_op jit(solution)/shard_map/reduce_scatter | solution.py:210
  182.9 14.1 %all-gather.10.cloned.1.call-done = bf16[1024,512]{1,0:T(8,128)(2,1)} async-done(((bf16[256,512]{1,0:T(8,128)(2,1)}), bf16[1024,512]{1,0:T(8,128)(2,1)}) %all-gather.10.cloned.1.call-update) | async-done | bytes 1048592 | tf_op jit(solution)/shard_map/all_gather | solution.py:129
  200.3 17.7 %all-gather.12.cloned.1.call-done = bf16[512,1536]{1,0:T(8,128)(2,1)} async-done(((bf16[128,1536]{1,0:T(8,128)(2,1)}), bf16[512,1536]{1,0:T(8,128)(2,1)}) %all-gather.12.cloned.1.call-update) | async-done | bytes 1572880 | tf_op jit(solution)/shard_map/all_gather | solution.py:130
  218.0 21.1 %all-gather.14.cloned.1.call-done = bf16[1536,512]{1,0:T(8,128)(2,1)} async-done(((bf16[384,512]{1,0:T(8,128)(2,1)}), bf16[1536,512]{1,0:T(8,128)(2,1)}) %all-gather.14.cloned.1.call-update) | async-done | bytes 1572880 | tf_op jit(solution)/shard_map/all_gather | solution.py:131
  239.1 4.3 %fusion.178 = (f32[132]{0:T(256)S(1)}, f32[132,512]{1,0:T(8,128)S(1)}) fusion(bf16[1536,512]{1,0:T(8,128)(2,1)} %all-gather.14.cloned.1.call-done, bf16[512,1536]{1,0:T(8,128)(2,1)} %all-gather.12.cloned.1.call-done, f32[132,512]{1,0:T(8,128)S(1)} %get-tuple-element.185, f32[132]{0:T(256)S(1)} %add_rsqrt_fusion.5, f32[132]{0:T(256)S(1)} %broadcast_multiply_fusion.4, ...), kind=kOutput, calls=%fused_computation.260 | convolution fusion | flops 428752768 | bytes 3958320 | tf_op jit(solution)/shard_map/dot_general | solution.py:229
  243.6 15.4 %all-gather.16.cloned.1.call-done = bf16[512,1282]{0,1:T(8,128)(2,1)} async-done(((bf16[128,1282]{0,1:T(8,128)(2,1)}), bf16[512,1282]{0,1:T(8,128)(2,1)}) %all-gather.16.cloned.1.call-update) | async-done | bytes 1312784 | tf_op jit(solution)/shard_map/all_gather | solution.py:132
  259.1 2.1 convolution_add_fusion
  261.2 1.9 cosine_multiply_fusion.1
  263.1 6.2 %fusion.19 = f32[132,1280]{1,0:T(8,128)S(1)} fusion(f32[641,1280]{1,0:T(8,128)S(1)} %copy-done.2, f32[641,1280]{1,0:T(8,128)} %get-tuple-element.254, f32[132,641]{1,0:T(8,128)S(1)} %get-tuple-element.199, f32[132,641]{1,0:T(8,128)S(1)} %get-tuple-element.198, f32[132]{0:T(256)S(1)} %and_convert_fusion, f32[1280]{0:T(1024)S(1)} %multiply_subtract_fusion), kind=kOutput, calls=%fused_computation.31 | convolution fusion | flops 2601428736 | bytes 7922224 | tf_op jit(solution)/shard_map/dot_general | solution.py:240
  (124 shorter events, 48.1 us)
Async XLA Ops:
  7.2 145.3 %copy-start = (bf16[256,1024]{1,0:T(8,128)(2,1)S(1)}, bf16[256,1024]{1,0:T(8,128)(2,1)}, u32[]{:S(2)}) copy-start(bf16[256,1024]{1,0:T(8,128)(2,1)} %param.29) | copy-start | bytes 1572868
  7.2 27.5 %all-gather.8.cloned.1.call-start = ((), (), s32[]{:S(2)}) async-start(), calls=%async_computation.1 | async-start | bytes 1310720 | tf_op jit(solution)/shard_map/all_gather | solution.py:128
  11.0 4.1 %copy-start.3 = (bf16[3,1024,128]{2,1,0:T(8,128)(2,1)S(1)}, bf16[3,1024,128]{2,1,0:T(8,128)(2,1)}, u32[]{:S(2)}) copy-start(bf16[3,1024,128]{2,1,0:T(8,128)(2,1)} %param.24) | copy-start | bytes 2359300
  14.9 117.1 %all-gather.18.cloned.1.call-start = ((), (), s32[]{:S(2)}) async-start(), calls=%async_computation.7 | async-start | bytes 5242880 | tf_op jit(solution)/shard_map/all_gather | solution.py:189
  34.6 3.2 %copy-start.1 = (bf16[512,1024]{1,0:T(8,128)(2,1)S(1)}, bf16[512,1024]{1,0:T(8,128)(2,1)}, u32[]{:S(2)}) copy-start(bf16[512,1024]{1,0:T(8,128)(2,1)} %all-gather.8.cloned.1.call-done) | copy-start | bytes 3145732
  61.4 18.3 %copy-start.8 = (f32[2]{0:T(128)S(1)}, f32[2]{0:T(128)}, u32[]{:S(2)}) copy-start(f32[2]{0:T(128)} %param.25) | copy-start | bytes 28
  95.3 2.5 copy-start.4
  97.7 81.1 %reduce-scatter.2.cloned.1.call-start = ((), (), s32[]{:S(2)}) async-start(), calls=%async_computation.2 | async-start | bytes 1474560 | tf_op jit(solution)/shard_map/reduce_scatter | solution.py:210
  136.4 12.1 %copy-start.7 = (bf16[2,1024,256]{2,1,0:T(8,128)(2,1)S(1)}, bf16[2,1024,256]{2,1,0:T(8,128)(2,1)}, u32[]{:S(2)}) copy-start(bf16[2,1024,256]{2,1,0:T(8,128)(2,1)} %param.27) | copy-start | bytes 3145732
  138.1 5.1 %collective-permute-start = (bf16[20,1024]{1,0:T(8,128)(2,1)S(1)}, bf16[20,1024]{1,0:T(8,128)(2,1)S(1)}, u32[]{:S(2)}, u32[]{:S(2)}) collective-permute-start(bf16[20,1024]{1,0:T(8,128)(2,1)S(1)} %get-tuple-element.190), channel_id=1, source_target_pairs={{0,4},{4,8},{8,12},{1,5},{5,9},{9,13},{2,6},{6,10},{10,14},{3,7},{... | collective-permute-start | bytes 122888 | tf_op jit(solution)/shard_map/ppermute | solution.py:17
  141.5 6.0 %collective-permute-start.1 = (bf16[20,1024]{1,0:T(8,128)(2,1)S(1)}, bf16[20,1024]{1,0:T(8,128)(2,1)S(1)}, u32[]{:S(2)}, u32[]{:S(2)}) collective-permute-start(bf16[20,1024]{1,0:T(8,128)(2,1)S(1)} %get-tuple-element.191), channel_id=1, source_target_pairs={{4,0},{8,4},{12,8},{5,1},{9,5},{13,9},{6,2},{10,6},{14,10},{7,3},{... | collective-permute-start | bytes 122888 | tf_op jit(solution)/shard_map/ppermute | solution.py:18
  152.4 4.8 %copy-start.5 = (f32[7,512]{1,0:T(8,128)S(1)}, f32[7,512]{1,0:T(8,128)}, u32[]{:S(2)}) copy-start(f32[7,512]{1,0:T(8,128)} %param.31) | copy-start | bytes 43012
  154.0 43.0 %all-gather.10.cloned.1.call-start = ((), (), s32[]{:S(2)}) async-start(), calls=%async_computation.3 | async-start | bytes 1310720 | tf_op jit(solution)/shard_map/all_gather | solution.py:129
  154.5 63.5 %all-gather.12.cloned.1.call-start = ((), (), s32[]{:S(2)}) async-start(), calls=%async_computation.4 | async-start | bytes 1966080 | tf_op jit(solution)/shard_map/all_gather | solution.py:130
  155.1 84.0 %all-gather.14.cloned.1.call-start = ((), (), s32[]{:S(2)}) async-start(), calls=%async_computation.5 | async-start | bytes 1966080 | tf_op jit(solution)/shard_map/all_gather | solution.py:131
  155.7 103.3 %all-gather.16.cloned.1.call-start = ((), (), s32[]{:S(2)}) async-start(), calls=%async_computation.6 | async-start | bytes 1648640 | tf_op jit(solution)/shard_map/all_gather | solution.py:132
  200.3 58.8 %copy-start.6 = (f32[1282]{0:T(1024)S(1)}, f32[1282]{0:T(1024)}, u32[]{:S(2)}) copy-start(f32[1282]{0:T(1024)} %param.35) | copy-start | bytes 15388
  259.1 4.0 %copy-start.2 = (f32[641,1280]{1,0:T(8,128)S(1)}, f32[641,1280]{1,0:T(8,128)}, u32[]{:S(2)}) copy-start(f32[641,1280]{1,0:T(8,128)} %get-tuple-element.253) | copy-start | bytes 9845764
Sparse Core Ops, SparseCore 0:
  15.1 19.5 all-gather.7
  97.8 34.1 all-gather.17
  154.1 24.6 reduce-scatter.1
  180.2 16.6 all-gather.9
  198.4 19.6 all-gather.11
  219.4 19.6 all-gather.13
  240.7 18.3 all-gather.15
